TPU v7x, 32 devices: a whole 2x2x4 slice. The times are simulated.
32 devices in a mesh: seq: 4 (over x, core), mp: 8 (over z, y).
Axes of the slice: x: 2, y: 2, z: 4, core: 2. Of those that a mesh axis runs over, the one named last changes fastest.
Arguments:
- queries: bfloat16 [1024, 4096], P('seq', 'mp'), may hold values from -15 to 15
- keys_values: bfloat16 [2, 1024, 4096], P(None, 'seq', 'mp'), may hold values from -6 to 6
- residual: bfloat16 [1024, 4096], P('seq', 'mp'), may hold values from -6 to 6
- cotangent: bfloat16 [1024, 4096], P('seq', 'mp'), may hold values from -6 to 6
- out_weight: bfloat16 [2, 4096, 4096], P(None, 'mp'), may hold values from -0.09375 to 0.09375
- kv_weight: bfloat16 [2, 4096, 4096], P(None, None, 'mp'), may hold values from -0.09375 to 0.09375
- bounds: int32 [2, 1024], replicated, may hold values from 0 to 767, as said below
- windows: int32 [64], P('mp'), may hold values from 1 to 127, as said below
Outputs:
- states_out: bfloat16 [1024, 4096], P('seq', 'mp')
- grad_states: bfloat16 [1024, 4096], P('seq', 'mp')
Inputs may be any that keep to these rules, and one draw needn't show every extreme that they name: The encoder rows form 4 documents, each a run of consecutive positions; an encoder token's bounds are its own document's first and last position. The last document begins among the last 255 encoder positions. Decoder tokens belong to documents in reverse order, the first decoder token to the last document (other documents may have none), and carry that document's encoder bounds. `windows`: some head reaches exactly 127.
All inputs are finite; a program needn't handle non-finite values.
Results may differ from a plain program's by a relative error of at most 0.038.
Values may be sent and summed in bfloat16 or wider, within the bound.
A program may use at most 64 MiB of HBM per device.

v0:
```python
import jax
import jax.numpy as jnp
from jax import lax
from jax.sharding import PartitionSpec as P

HD = 64
WIN = 127


def with_halo(cells, sides, width):
    for axis, dim in sides:
        count = lax.axis_size(axis)
        ends = count - 1
        head = lax.slice_in_dim(cells, 0, width, axis=dim)
        tail = lax.slice_in_dim(cells, cells.shape[dim] - width, cells.shape[dim], axis=dim)
        cells = jnp.concatenate(
            [
                lax.ppermute(tail, axis, [(i, (i + 1) % count) for i in range(ends)]),
                cells,
                lax.ppermute(head, axis, [((i + 1) % count, i) for i in range(ends)]),
            ],
            axis=dim,
        )
    return cells


def softmax_masked(scores, permitted):
    masked_scores = jnp.where(permitted, scores, -jnp.inf)
    row_top = jnp.max(masked_scores, axis=-1, keepdims=True)
    exp_scores = jnp.exp(masked_scores - row_top)
    return exp_scores / jnp.sum(exp_scores, axis=-1, keepdims=True)


def shards(queries, keys_values, residual, cotangent, out_weight, kv_weight, bounds, windows):
    row_count = queries.shape[0]
    col_count = queries.shape[1]
    head_count = col_count // HD
    slab_count = lax.axis_size("seq")
    enc_slabs = 3 * slab_count // 4
    dec_slabs = slab_count - enc_slabs
    enc_tokens = enc_slabs * row_count
    token_count = slab_count * row_count
    dec_tokens = token_count - enc_tokens
    slab_index = lax.axis_index("seq")
    is_enc = slab_index < enc_slabs
    score_scale = HD ** (-0.5)
    own_pos = slab_index * row_count + jnp.arange(row_count, dtype=jnp.int32)
    own_first = lax.dynamic_slice_in_dim(bounds[0], slab_index * row_count, row_count)
    own_last = lax.dynamic_slice_in_dim(bounds[1], slab_index * row_count, row_count)
    query_heads = queries.reshape(row_count, head_count, HD)
    slice_cols = residual.shape[1]
    res_full, cot_full = (
        lax.all_gather(residual, "mp", axis=1, tiled=True),
        lax.all_gather(cotangent, "mp", axis=1, tiled=True),
    )
    model_width = cot_full.shape[1]
    rim_keys = with_halo(keys_values, (("seq", 1),), WIN)

    def local_part():
        span_count = rim_keys.shape[1]
        key_pos = slab_index * row_count - WIN + jnp.arange(span_count, dtype=jnp.int32)
        key_heads = rim_keys[0].reshape(span_count, head_count, HD)
        value_heads = rim_keys[1].reshape(span_count, head_count, HD)
        scores = (
            jnp.einsum("qhd,khd->hqk", query_heads, key_heads, preferred_element_type=jnp.float32)
            * score_scale
        )
        in_document = (key_pos[None, :] >= own_first[:, None]) & (
            key_pos[None, :] <= own_last[:, None]
        )
        distance = jnp.abs(own_pos[:, None] - key_pos[None, :])
        permitted = in_document[None] & (distance[None] <= windows[:, None, None])
        rounded = softmax_masked(scores, permitted).astype(jnp.bfloat16)
        context = jnp.einsum(
            "hqk,khd->qhd", rounded, value_heads, preferred_element_type=jnp.float32
        ).astype(jnp.bfloat16)
        return jnp.dot(
            context.reshape(row_count, col_count), out_weight[0], preferred_element_type=jnp.float32
        )

    head_partial = lax.cond(
        is_enc, local_part, lambda: jnp.zeros((row_count, model_width), jnp.float32)
    )
    attn_sum = lax.psum(head_partial.astype(jnp.bfloat16), "mp").astype(jnp.float32)
    hidden_full = (res_full.astype(jnp.float32) + attn_sum).astype(jnp.bfloat16)
    encoder_out = lax.dynamic_slice_in_dim(
        hidden_full, lax.axis_index("mp") * slice_cols, slice_cols, 1
    )

    def project_keys():
        key_proj = jnp.dot(hidden_full, kv_weight[0], preferred_element_type=jnp.float32).astype(
            jnp.bfloat16
        )
        value_proj = jnp.dot(hidden_full, kv_weight[1], preferred_element_type=jnp.float32).astype(
            jnp.bfloat16
        )
        return jnp.stack([key_proj, value_proj])

    cross_kv = lax.cond(
        is_enc, project_keys, lambda: jnp.zeros((2, row_count, col_count), jnp.bfloat16)
    )

    def context_gradient():
        return lax.dot_general(
            cot_full, out_weight[1], (((1,), (1,)), ((), ())), preferred_element_type=jnp.float32
        ).astype(jnp.bfloat16)

    dec_queries = lax.all_gather(queries, "seq", axis=0, tiled=True)[enc_tokens:]
    dec_heads = dec_queries.reshape(dec_tokens, head_count, HD)
    dec_first = bounds[0, enc_tokens:]
    dec_last = bounds[1, enc_tokens:]
    in_document = (own_pos[None, :] >= dec_first[:, None]) & (own_pos[None, :] <= dec_last[:, None])
    key_heads = cross_kv[0].reshape(row_count, head_count, HD)
    value_heads = cross_kv[1].reshape(row_count, head_count, HD)
    scores = (
        jnp.einsum("qhd,khd->hqk", dec_heads, key_heads, preferred_element_type=jnp.float32)
        * score_scale
    )
    masked_scores = jnp.where(in_document[None], scores, -jnp.inf)
    row_top = lax.pmax(jnp.max(masked_scores, axis=2), "seq")
    exp_scores = jnp.exp(masked_scores - row_top[:, :, None])
    row_total = lax.psum(jnp.sum(exp_scores, axis=2), "seq")
    weights = exp_scores / row_total[:, :, None]
    rounded = weights.astype(jnp.bfloat16)
    partial_ctx = jnp.einsum(
        "hqk,khd->qhd", rounded, value_heads, preferred_element_type=jnp.float32
    ).reshape(dec_tokens, col_count)
    context_all = lax.psum(partial_ctx.astype(jnp.bfloat16), "seq")
    dec_offset = jnp.maximum(slab_index - enc_slabs, 0) * row_count
    context = lax.dynamic_slice_in_dim(context_all, dec_offset, row_count, 0)
    out_part = lax.cond(
        is_enc,
        lambda: jnp.zeros((row_count, model_width), jnp.float32),
        lambda: jnp.dot(context, out_weight[1], preferred_element_type=jnp.float32),
    )
    grad_own = lax.cond(
        is_enc, lambda: jnp.zeros((row_count, col_count), jnp.bfloat16), context_gradient
    )
    grad_all = lax.all_gather(grad_own, "seq", axis=0, tiled=True)[enc_tokens:]
    grad_heads = grad_all.reshape(dec_tokens, head_count, HD)
    row_dots = jnp.einsum(
        "qhd,qhd->hq",
        grad_heads,
        context_all.reshape(dec_tokens, head_count, HD),
        preferred_element_type=jnp.float32,
    )
    prob_grad = jnp.einsum(
        "qhd,khd->hqk", grad_heads, value_heads, preferred_element_type=jnp.float32
    )
    score_grad = (weights * (prob_grad - row_dots[:, :, None])).astype(jnp.bfloat16)
    grad_blocks = score_grad.reshape(head_count, dec_slabs, row_count, row_count)
    prob_blocks = rounded.reshape(head_count, dec_slabs, row_count, row_count)
    query_blocks = dec_heads.reshape(dec_slabs, row_count, head_count, HD)
    grad_rows = grad_heads.reshape(dec_slabs, row_count, head_count, HD)
    key_parts = (
        score_scale
        * jnp.einsum(
            "hsqk,sqhd->skhd", grad_blocks, query_blocks, preferred_element_type=jnp.float32
        )
    ).astype(jnp.bfloat16)
    value_parts = jnp.einsum(
        "hsqk,sqhd->skhd", prob_blocks, grad_rows, preferred_element_type=jnp.float32
    ).astype(jnp.bfloat16)
    key_grad = (
        jnp.sum(key_parts.astype(jnp.float32), axis=0)
        .astype(jnp.bfloat16)
        .reshape(row_count, col_count)
    )
    value_grad = (
        jnp.sum(value_parts.astype(jnp.float32), axis=0)
        .astype(jnp.bfloat16)
        .reshape(row_count, col_count)
    )
    query_terms = score_scale * jnp.einsum(
        "hqk,khd->qhd", score_grad, key_heads, preferred_element_type=jnp.float32
    )
    query_sum = lax.psum(
        query_terms.reshape(dec_tokens, col_count).astype(jnp.bfloat16), "seq"
    ).astype(jnp.float32)
    query_grad = lax.dynamic_slice_in_dim(query_sum, dec_offset, row_count, 0).astype(jnp.bfloat16)
    contract = (((1,), (1,)), ((), ()))
    grad_terms = lax.dot_general(
        key_grad, kv_weight[0], contract, preferred_element_type=jnp.float32
    ) + lax.dot_general(value_grad, kv_weight[1], contract, preferred_element_type=jnp.float32)
    final_term = jnp.where(is_enc, grad_terms, out_part)
    final_share = lax.psum_scatter(
        final_term.astype(jnp.bfloat16), "mp", scatter_dimension=1, tiled=True
    ).astype(jnp.float32)
    base_rows = jnp.where(is_enc, cotangent, residual).astype(jnp.float32)
    final_rows = (base_rows + final_share).astype(jnp.bfloat16)
    states_out = jnp.where(is_enc, encoder_out, final_rows)
    grad_states = jnp.where(is_enc, final_rows, query_grad)
    return (states_out, grad_states)


def solution(mesh):
    return jax.shard_map(
        shards,
        mesh=mesh,
        in_specs=(
            P("seq", "mp"),
            P(None, "seq", "mp"),
            P("seq", "mp"),
            P("seq", "mp"),
            P(None, "mp", None),
            P(None, None, "mp"),
            P(),
            P("mp"),
        ),
        out_specs=(P("seq", "mp"), P("seq", "mp")),
        check_vma=False,
    )
```

profile of v0, /device:TPU:0, one launch (start us, length us, event | category | flops | bytes accessed | tf_op | source)
XLA Modules:
  0.0 340.2 jit_solution(7236549203202645054)
XLA Ops:
  8.8 1.2 copy.30
  10.2 2.4 collective-permute-start
  12.6 1.3 collective-permute-start.1
  13.9 4.2 %collective-permute-done.1 = bf16[2,127,512]{1,2,0:T(8,128)(2,1)S(1)} collective-permute-done((bf16[2,127,512]{1,2,0:T(8,128)(2,1)S(1)}, bf16[2,127,512]{1,2,0:T(8,128)(2,1)S(1)}, u32[]{:S(2)}, u32[]{:S(2)}) %collective-permute-start.1) | collective-permute-done | bytes 260128 | tf_op jit(solution)/shard_map/ppermute | solution.py:20
  18.7 8.5 %conditional.4 = (bf16[256,4096]{1,0:T(8,128)(2,1)S(1)}) conditional(s32[]{:T(128)} %convert_element_type.116, () %tuple.47, (s32[]{:T(128)}, s32[2,1024]{1,0:T(2,128)S(1)}, s32[]{:T(128)}, s32[256]{0:T(256)S(1)}, s32[8]{0:T(128)S(1)}, /*index=5*/bf16[256,512]{1,0:T(8,128)(2,1)S(1)}, bf16[2,510,512]{1,2,0:T(8,128)(2,1)S(1)}, ...), branch_computations={%region_0.0_spmd, %region_1.4_spmd} | conditional | flops 1489188096 | bytes 13526646 | solution.py:81
  19.4 2.0 fusion.56
  21.5 2.3 fusion.11
  23.7 3.5 %fusion.1 = bf16[256,4096]{1,0:T(8,128)(2,1)S(1)} fusion(bf16[256,512]{0,1:T(8,128)(2,1)S(1)} %bitcast.107, bf16[2,512,4096]{2,1,0:T(8,128)(2,1)} %get-tuple-element.145), kind=kOutput, calls=%fused_computation.1 | convolution fusion | flops 1073741824 | bytes 6553600 | tf_op jit(solution)/shard_map/cond/branch_1_fun/dot_general | solution.py:77
  27.2 1.3 copy-done.2
  31.4 136.0 %all-reduce.4.cloned.1.call-done = bf16[256,4096]{1,0:T(8,128)(2,1)} async-done(((bf16[256,4096]{1,0:T(8,128)(2,1)}), bf16[256,4096]{1,0:T(8,128)(2,1)}) %all-reduce.4.cloned.1.call-update) | async-done | bytes 2097168 | tf_op jit(solution)/shard_map/psum | solution.py:84
  167.4 4.3 %add_convert_fusion = bf16[256,4096]{1,0:T(8,128)(2,1)} fusion(bf16[256,4096]{1,0:T(8,128)(2,1)} %all-reduce.4.cloned.1.call-done, bf16[256,4096]{1,0:T(8,128)(2,1)} %all-gather.5.cloned.1.call-done), kind=kLoop, calls=%fused_computation.49 | loop fusion | flops 4194304 | bytes 6291456 | tf_op jit(solution)/shard_map/convert_element_type | solution.py:85
  171.8 8.3 %conditional.5 = (bf16[256,8,64]{0,2,1:T(8,128)(2,1)S(1)}, bf16[256,8,64]{0,2,1:T(8,128)(2,1)S(1)}) conditional(s32[]{:T(128)} %convert_element_type.116, () %tuple.49, (bf16[2,4096,512]{2,1,0:T(8,128)(2,1)}, bf16[256,4096]{1,0:T(8,128)(2,1)}) %tuple.50), branch_computations={%region_5.6_spmd, %region_6.7_spmd} | conditional | flops 2147745792 | bytes 47710252 | solution.py:99
  171.8 4.2 %fusion.29 = bf16[256,512]{1,0:T(8,128)(2,1)S(1)} fusion(bf16[256,4096]{1,0:T(8,128)(2,1)} %get-tuple-element.146, bf16[2,4096,512]{2,1,0:T(8,128)(2,1)} %get-tuple-element.147), kind=kOutput, calls=%fused_computation.33 | convolution fusion | flops 1073872896 | bytes 6553600 | tf_op jit(solution)/shard_map/cond/branch_1_fun/dot_general | solution.py:94
  176.0 1.0 copy-done.1
  177.0 2.8 fusion.26
  180.7 5.8 %pmax.7 = f32[8,256]{1,0:T(8,128)S(1)} all-reduce(f32[8,256]{1,0:T(8,128)S(1)} %get-tuple-element.190), channel_id=1, replica_groups=mesh['seq'=4,'mp'=8] {'seq'}, use_global_device_ids=true, to_apply=%region_8.9 | all-reduce | flops 2048 | bytes 16384 | tf_op jit(solution)/shard_map/pmax | solution.py:120
  186.7 6.7 %psum.29 = f32[8,256]{1,0:T(8,128)S(1)} all-reduce(f32[8,256]{1,0:T(8,128)S(1)} %fusion.49), channel_id=1, replica_groups=mesh['seq'=4,'mp'=8] {'seq'}, use_global_device_ids=true, to_apply=%region_10.11 | all-reduce | flops 2048 | bytes 16384 | tf_op jit(solution)/shard_map/psum | solution.py:122
  193.7 1.0 convolution_convert_fusion.1
  195.9 29.9 %all-reduce.6.cloned.1.call-done = bf16[256,512]{0,1:T(8,128)(2,1)} async-done(((bf16[256,512]{0,1:T(8,128)(2,1)}), bf16[256,512]{0,1:T(8,128)(2,1)}) %all-reduce.6.cloned.1.call-update) | async-done | bytes 262160 | tf_op jit(solution)/shard_map/psum | solution.py:128
  225.8 1.5 conditional.7
  225.8 1.5 broadcast.157
  227.3 17.2 %all-gather.11.cloned.1.call-done = bf16[1024,512]{1,0:T(8,128)(2,1)} async-done(((bf16[256,512]{1,0:T(8,128)(2,1)}), bf16[1024,512]{1,0:T(8,128)(2,1)}) %all-gather.11.cloned.1.call-update) | async-done | bytes 1048592 | tf_op jit(solution)/shard_map/all_gather | solution.py:139
  244.5 1.7 slice.91
  246.2 1.1 copy.35
  247.3 1.1 convolution_convert_fusion
  248.4 1.0 fusion.53
  249.5 1.7 multiply_convert_fusion
  252.9 3.6 %fusion.44 = f32[256,4096]{1,0:T(8,128)S(1)} fusion(bf16[256,512]{0,1:T(8,128)(2,1)S(1)} %bitcast.100, bf16[2,4096,512]{2,1,0:T(8,128)(2,1)} %param.21), kind=kOutput, calls=%fused_computation.45 | convolution fusion | flops 1073741824 | bytes 8650752 | tf_op jit(solution)/shard_map/dot_general | solution.py:182
  256.6 5.0 %fusion.42 = bf16[256,4096]{1,0:T(8,128)(2,1)} fusion(bf16[256,4096]{1,0:T(8,128)(2,1)S(1)} %copy-done, f32[256,4096]{1,0:T(8,128)S(1)} %fusion.44, bf16[256,512]{0,1:T(8,128)(2,1)S(1)} %bitcast.99, bf16[2,4096,512]{2,1,0:T(8,128)(2,1)} %param.21, pred[]{:T(512)S(6)} %lt.14), kind=kOutput, calls=%fused_computation.43 | convolution fusion | flops 1075838976 | bytes 12845057 | tf_op jit(solution)/shard_map/dot_general | solution.py:184
  261.6 23.6 %all-reduce.8.cloned.1.call-done = bf16[256,512]{1,0:T(8,128)(2,1)} async-done(((bf16[256,512]{1,0:T(8,128)(2,1)}), bf16[256,512]{1,0:T(8,128)(2,1)}) %all-reduce.8.cloned.1.call-update) | async-done | bytes 262160 | tf_op jit(solution)/shard_map/psum | solution.py:177
  285.2 45.5 %reduce-scatter.2.cloned.1.call-done = bf16[256,512]{1,0:T(8,128)(2,1)} async-done(((bf16[256,4096]{1,0:T(8,128)(2,1)}), bf16[256,512]{1,0:T(8,128)(2,1)}) %reduce-scatter.2.cloned.1.call-update) | async-done | bytes 262160 | tf_op jit(solution)/shard_map/reduce_scatter | solution.py:186
  330.8 2.0 broadcast_select_fusion
  (74 shorter events, 9.0 us)
Async XLA Ops:
  8.0 10.7 %copy-start.9 = (bf16[256,512]{1,0:T(8,128)(2,1)S(1)}, bf16[256,512]{1,0:T(8,128)(2,1)}, u32[]{:S(2)}) copy-start(bf16[256,512]{1,0:T(8,128)(2,1)} %param.16) | copy-start | bytes 786436
  8.0 10.7 %copy-start.13 = (s32[2,1024]{1,0:T(2,128)S(1)}, s32[2,1024]{1,0:T(2,128)}, u32[]{:S(2)}) copy-start(s32[2,1024]{1,0:T(2,128)} %param.22) | copy-start | bytes 24580
  8.0 10.7 %copy-start.14 = (s32[8]{0:T(128)S(1)}, s32[8]{0:T(128)}, u32[]{:S(2)}) copy-start(s32[8]{0:T(128)} %param.23) | copy-start | bytes 100
  8.0 22.3 %all-gather.7.cloned.1.call-start = ((), (), s32[]{:S(2)}) async-start(), calls=%async_computation.3 | async-start | bytes 1310720 | tf_op jit(solution)/shard_map/all_gather | solution.py:108
  8.8 158.6 %all-reduce.4.cloned.1.call-start = ((), (), s32[]{:S(2)}) async-start(), calls=%async_computation.2 | async-start | bytes 4194304 | tf_op jit(solution)/shard_map/psum | solution.py:84
  10.2 3.7 %collective-permute-start = (bf16[2,127,512]{1,2,0:T(8,128)(2,1)S(1)}, bf16[2,127,512]{1,2,0:T(8,128)(2,1)S(1)}, u32[]{:S(2)}, u32[]{:S(2)}) collective-permute-start(bf16[2,127,512]{1,2,0:T(8,128)(2,1)S(1)} %get-tuple-element.186), channel_id=1, source_target_pairs={{0,8},{8,16},{16,24},{1,9},{9,17},{17,25},{2,10},{10,18},{18,26},{... | collective-permute-start | bytes 780296 | tf_op jit(solution)/shard_map/ppermute | solution.py:18
  12.6 5.5 %collective-permute-start.1 = (bf16[2,127,512]{1,2,0:T(8,128)(2,1)S(1)}, bf16[2,127,512]{1,2,0:T(8,128)(2,1)S(1)}, u32[]{:S(2)}, u32[]{:S(2)}) collective-permute-start(bf16[2,127,512]{1,2,0:T(8,128)(2,1)S(1)} %get-tuple-element.187), channel_id=1, source_target_pairs={{8,0},{16,8},{24,16},{9,1},{17,9},{25,17},{10,2},{18,10},{26,18},{... | collective-permute-start | bytes 780296 | tf_op jit(solution)/shard_map/ppermute | solution.py:20
  27.2 1.3 copy-start.2
  28.6 138.8 %all-gather.5.cloned.1.call-start = ((), (), s32[]{:S(2)}) async-start(), calls=%async_computation.1 | async-start | bytes 2359296 | tf_op jit(solution)/shard_map/all_gather | solution.py:53
  29.4 165.5 %all-gather.9.cloned.1.call-start = ((), (), s32[]{:S(2)}) async-start(), calls=%async_computation.4 | async-start | bytes 2359296 | tf_op jit(solution)/shard_map/all_gather | solution.py:54
  30.1 195.7 %all-reduce.6.cloned.1.call-start = ((), (), s32[]{:S(2)}) async-start(), calls=%async_computation.6 | async-start | bytes 524288 | tf_op jit(solution)/shard_map/psum | solution.py:128
  31.4 148.7 %copy-start.3 = (bf16[256,512]{0,1:T(8,128)(2,1)}, bf16[256,512]{0,1:T(8,128)(2,1)S(1)}, u32[]{:S(2)}) copy-start(bf16[256,512]{0,1:T(8,128)(2,1)S(1)} %copy.34) | copy-start | bytes 786436
  171.8 5.2 %copy-start.1 = (bf16[2,4096,512]{2,1,0:T(8,128)(2,1)S(1)}, bf16[2,4096,512]{2,1,0:T(8,128)(2,1)}, u32[]{:S(2)}) copy-start(bf16[2,4096,512]{2,1,0:T(8,128)(2,1)} %get-tuple-element.147) | copy-start | bytes 25165828 | tf_op jit(solution)/shard_map/cond
  180.1 6.6 %copy-start.5 = (bf16[256,8,64]{0,2,1:T(8,128)(2,1)}, bf16[256,8,64]{0,2,1:T(8,128)(2,1)S(1)}, u32[]{:S(2)}) copy-start(bf16[256,8,64]{0,2,1:T(8,128)(2,1)S(1)} %get-tuple-element.156) | copy-start | bytes 786436
  180.1 14.6 %copy-start.11 = (bf16[256,8,64]{0,2,1:T(8,128)(2,1)}, bf16[256,8,64]{0,2,1:T(8,128)(2,1)S(1)}, u32[]{:S(2)}) copy-start(bf16[256,8,64]{0,2,1:T(8,128)(2,1)S(1)} %get-tuple-element.157) | copy-start | bytes 786436
  194.8 49.7 %all-gather.11.cloned.1.call-start = ((), (), s32[]{:S(2)}) async-start(), calls=%async_computation.5 | async-start | bytes 1310720 | tf_op jit(solution)/shard_map/all_gather | solution.py:139
  195.1 0.7 copy-start.12
  195.8 89.4 %all-reduce.8.cloned.1.call-start = ((), (), s32[]{:S(2)}) async-start(), calls=%async_computation.8 | async-start | bytes 524288 | tf_op jit(solution)/shard_map/psum | solution.py:177
  249.5 1.7 copy-start.6
  249.5 2.0 copy-start.4
  252.8 78.0 %reduce-scatter.2.cloned.1.call-start = ((), (), s32[]{:S(2)}) async-start(), calls=%async_computation.7 | async-start | bytes 2359296 | tf_op jit(solution)/shard_map/reduce_scatter | solution.py:186
  252.8 3.7 %copy-start = (bf16[256,4096]{1,0:T(8,128)(2,1)S(1)}, bf16[256,4096]{1,0:T(8,128)(2,1)}, u32[]{:S(2)}) copy-start(bf16[256,4096]{1,0:T(8,128)(2,1)} %get-tuple-element.198) | copy-start | bytes 6291460
  252.8 3.7 %copy-start.10 = (bf16[8,64,256]{2,1,0:T(8,128)(2,1)S(1)}, bf16[8,64,256]{2,1,0:T(8,128)(2,1)}, u32[]{:S(2)}) copy-start(bf16[8,64,256]{2,1,0:T(8,128)(2,1)} %convolution_convert_fusion) | copy-start | bytes 786436
  256.5 74.2 %copy-start.7 = (bf16[256,512]{1,0:T(8,128)(2,1)S(1)}, bf16[256,512]{1,0:T(8,128)(2,1)}, u32[]{:S(2)}) copy-start(bf16[256,512]{1,0:T(8,128)(2,1)} %param.18) | copy-start | bytes 786436
  256.5 74.2 %copy-start.8 = (bf16[256,512]{1,0:T(8,128)(2,1)S(1)}, bf16[256,512]{1,0:T(8,128)(2,1)}, u32[]{:S(2)}) copy-start(bf16[256,512]{1,0:T(8,128)(2,1)} %param.19) | copy-start | bytes 786436
Sparse Core Ops, SparseCore 0:
  10.4 19.7 all-gather.6
  32.2 71.5 all-gather.4
  105.9 66.6 all-gather.8
  194.9 30.8 all-reduce.5
  227.8 16.6 all-gather.10
  252.9 32.2 all-reduce.7
Sparse Core Ops, SparseCore 1:
  28.7 138.7 all-reduce.3
  261.7 69.0 reduce-scatter.1
where the time goes:
time: 341 us; the launch traced here: 340 us
  waiting for transfers between devices  259 us (76%)
  matrix products  28.6 us (8%)
  between operations  15.9 us (5%)
  blocking collectives  12.4 us (4%)
  local copies, waits for them, and re-layouts  11.3 us (3%)
  other arithmetic  8.97 us (3%)
  starting transfers between devices  4.03 us (1%)
    psum x1, waiting for transfers between devices, shards(): lax.psum(head_partial.astype(jnp.bfloat16), 'mp').astype(jnp.float32)  136 us
    reduce_scatter x1, waiting for transfers between devices, shards(): lax.psum_scatter(final_term.astype(jnp.bfloat16), 'mp', scatter_dimension...  45.5 us
    psum x1, waiting for transfers between devices, shards(): context_all = lax.psum(partial_ctx.astype(jnp.bfloat16), 'seq')  29.9 us
    psum x1, waiting for transfers between devices, shards(): lax.psum(query_terms.reshape(dec_tokens, col_count).astype(jnp.bfloat16),...  23.6 us
    all_gather x1, waiting for transfers between devices, shards(): grad_all = lax.all_gather(grad_own, 'seq', axis=0, tiled=True)[enc_tokens:]  17.2 us
  transfers between devices with their start and end apart: 10, of which 6 were waited for; matrix products, arithmetic and copies ran while one was open for 10% of the time, Pallas kernels for 0%

commit v1 on v0

--- a/solution.py
+++ b/solution.py
@@ -5,6 +5,27 @@
 
 HD = 64
 WIN = 127
+
+
+def collect(shard, axis, dim):
+    size, place, span = (lax.axis_size(axis), lax.axis_index(axis), shard.shape[dim])
+    right = [(i, (i + 1) % size) for i in range(size)]
+    downward = [(i, (i - 1) % size) for i in range(size)]
+    out = jnp.zeros((*shard.shape[:dim], size * span, *shard.shape[dim + 1 :]), shard.dtype)
+    out = lax.dynamic_update_slice_in_dim(out, shard, place * span, axis=dim)
+    from_left = from_right = shard
+    half = size // 2
+    for step in range(1, half + 1):
+        from_left = lax.ppermute(from_left, axis, right)
+        out = lax.dynamic_update_slice_in_dim(
+            out, from_left, (place - step) % size * span, axis=dim
+        )
+        if step < size - half:
+            from_right = lax.ppermute(from_right, axis, downward)
+            out = lax.dynamic_update_slice_in_dim(
+                out, from_right, (place + step) % size * span, axis=dim
+            )
+    return out
 
 
 def with_halo(cells, sides, width):
@@ -136,7 +157,7 @@
     grad_own = lax.cond(
         is_enc, lambda: jnp.zeros((row_count, col_count), jnp.bfloat16), context_gradient
     )
-    grad_all = lax.all_gather(grad_own, "seq", axis=0, tiled=True)[enc_tokens:]
+    grad_all = collect(grad_own, "seq", 0)[enc_tokens:]
     grad_heads = grad_all.reshape(dec_tokens, head_count, HD)
     row_dots = jnp.einsum(
         "qhd,qhd->hq",

time: 341 us -> 431 us (1.26)
  waiting for transfers between devices: 259 us -> 333 us
  local copies, waits for them, and re-layouts: 11.3 us -> 23.7 us
    all_gather x1, waiting for transfers between devices: 0.02 us -> 51.6 us  [shards(): lax.all_gather(cotangent, 'mp', axis=1, tiled=True)]
    all_gather x1, waiting for transfers between devices: 0.01 us -> 51.6 us  [shards(): lax.all_gather(residual, 'mp', axis=1, tiled=True)]
    psum x1, waiting for transfers between devices: 136 us -> 99.1 us  [shards(): lax.psum(head_partial.astype(jnp.bfloat16), 'mp').astype(jnp.float32)]
    reduce_scatter x1, waiting for transfers between devices: 45.5 us -> 72.4 us  [shards(): lax.psum_scatter(final_term.astype(jnp.bfloat16), 'mp', scatter_dimension...]
    all_gather x1 -> x0, waiting for transfers between devices: 17.2 us -> none  [shards(): grad_all = lax.all_gather(grad_own, 'seq', axis=0, tiled=True)[enc_tokens:]]
    dynamic_update_slice x0 -> x4, local copies, waits for them, and re-layouts: none -> 6.8 us  [the longest x2 3.41 us: collect(): lax.dynamic_update_slice_in_dim(out, from_left, (place - step) % size * s...]
    ppermute x0 -> x3, local copies, waits for them, and re-layouts: none -> 5.41 us  [the longest x2 3.61 us: collect(): from_left = lax.ppermute(from_left, axis, right)]
    psum x1, waiting for transfers between devices: 29.9 us -> 25.4 us  [shards(): context_all = lax.psum(partial_ctx.astype(jnp.bfloat16), 'seq')]
  transfers between devices with their start and end apart: 10 -> 12, of which waited for: 6 -> 8; matrix products, arithmetic and copies ran while one was open for 10% -> 11% of each run, Pallas kernels for 0% -> 0%
where the time goes in v1:
time: 431 us
  waiting for transfers between devices  333 us (77%)
  matrix products  29.5 us (7%)
  local copies, waits for them, and re-layouts  23.7 us (5%)
  between operations  14.5 us (3%)
  blocking collectives  12.5 us (3%)
  other arithmetic  9.06 us (2%)
  starting transfers between devices  8.27 us (2%)
    psum x1, waiting for transfers between devices, shards(): lax.psum(head_partial.astype(jnp.bfloat16), 'mp').astype(jnp.float32)  99.1 us
    reduce_scatter x1, waiting for transfers between devices, shards(): lax.psum_scatter(final_term.astype(jnp.bfloat16), 'mp', scatter_dimension...  72.4 us
    all_gather x1, waiting for transfers between devices, shards(): lax.all_gather(cotangent, 'mp', axis=1, tiled=True)  51.6 us
    all_gather x1, waiting for transfers between devices, shards(): lax.all_gather(residual, 'mp', axis=1, tiled=True)  51.6 us
    psum x1, waiting for transfers between devices, shards(): lax.psum(query_terms.reshape(dec_tokens, col_count).astype(jnp.bfloat16),...  25.7 us
    psum x1, waiting for transfers between devices, shards(): context_all = lax.psum(partial_ctx.astype(jnp.bfloat16), 'seq')  25.4 us
  transfers between devices with their start and end apart: 12, of which 8 were waited for; matrix products, arithmetic and copies ran while one was open for 11% of the time, Pallas kernels for 0%

profile of v1, /device:TPU:0, one launch (start us, length us, event | category | flops | bytes accessed | tf_op | source)
XLA Modules:
  0.0 430.7 jit_solution(17019012001093195140)
XLA Ops:
  10.1 2.4 collective-permute-start
  13.9 4.2 collective-permute-done.1
  18.6 8.5 %conditional.4 = (bf16[256,4096]{1,0:T(8,128)(2,1)S(1)}) conditional(s32[]{:T(128)} %convert_element_type.114, () %tuple.44, (s32[]{:T(128)}, s32[2,1024]{1,0:T(2,128)S(1)}, s32[]{:T(128)}, s32[]{:T(128)}, s32[256]{0:T(256)S(1)}, /*index=5*/s32[8]{0:T(128)S(1)}, bf16[256,512]{1,0:T(8,128)(2,1)S(1)}, bf16[2,510,512]{1,2,0:T(8,128)(2,1)S(1)}, ...), branch_computations={%region_0.0_spmd, %region_1.4_spmd} | conditional | flops 1489188096 | bytes 13526612 | solution.py:102
  19.3 2.0 fusion.56
  21.4 2.3 fusion.11
  23.7 3.5 fusion.1
  31.2 51.6 %all-gather.8.cloned.1.call-done = bf16[256,4096]{1,0:T(8,128)(2,1)} async-done(((bf16[256,512]{1,0:T(8,128)(2,1)}), bf16[256,4096]{1,0:T(8,128)(2,1)}) %all-gather.8.cloned.1.call-update) | async-done | bytes 2097168 | tf_op jit(solution)/shard_map/all_gather | solution.py:75
  83.6 4.3 collective-permute-start.3
  87.9 99.1 %all-reduce.4.cloned.1.call-done = bf16[256,4096]{1,0:T(8,128)(2,1)} async-done(((bf16[256,4096]{1,0:T(8,128)(2,1)}), bf16[256,4096]{1,0:T(8,128)(2,1)}) %all-reduce.4.cloned.1.call-update) | async-done | bytes 2097168 | tf_op jit(solution)/shard_map/psum | solution.py:105
  187.0 51.6 %all-gather.4.cloned.1.call-done = bf16[256,4096]{1,0:T(8,128)(2,1)} async-done(((bf16[256,512]{1,0:T(8,128)(2,1)}), bf16[256,4096]{1,0:T(8,128)(2,1)}) %all-gather.4.cloned.1.call-update) | async-done | bytes 2097168 | tf_op jit(solution)/shard_map/all_gather | solution.py:74
  238.5 4.3 %add_convert_fusion = bf16[256,4096]{1,0:T(8,128)(2,1)} fusion(bf16[256,4096]{1,0:T(8,128)(2,1)} %all-reduce.4.cloned.1.call-done, bf16[256,4096]{1,0:T(8,128)(2,1)} %all-gather.4.cloned.1.call-done), kind=kLoop, calls=%fused_computation.49 | loop fusion | flops 4194304 | bytes 6291456 | tf_op jit(solution)/shard_map/convert_element_type | solution.py:106
  242.9 8.5 %conditional.5 = (bf16[256,8,64]{0,2,1:T(8,128)(2,1)S(1)}, bf16[256,8,64]{0,2,1:T(8,128)(2,1)S(1)}) conditional(s32[]{:T(128)} %convert_element_type.114, () %tuple.46, (bf16[2,4096,512]{2,1,0:T(8,128)(2,1)}, bf16[256,4096]{1,0:T(8,128)(2,1)}) %tuple.47), branch_computations={%region_5.6_spmd, %region_6.7_spmd} | conditional | flops 2147745792 | bytes 47710252 | solution.py:120
  242.9 4.2 fusion.29
  248.1 2.8 fusion.26
  251.9 5.8 %pmax.7 = f32[8,256]{1,0:T(8,128)S(1)} all-reduce(f32[8,256]{1,0:T(8,128)S(1)} %get-tuple-element.164), channel_id=1, replica_groups=mesh['seq'=4,'mp'=8] {'seq'}, use_global_device_ids=true, to_apply=%region_8.9 | all-reduce | flops 2048 | bytes 16384 | tf_op jit(solution)/shard_map/pmax | solution.py:141
  258.0 6.7 %psum.29 = f32[8,256]{1,0:T(8,128)S(1)} all-reduce(f32[8,256]{1,0:T(8,128)S(1)} %fusion.49), channel_id=1, replica_groups=mesh['seq'=4,'mp'=8] {'seq'}, use_global_device_ids=true, to_apply=%region_10.11 | all-reduce | flops 2048 | bytes 16384 | tf_op jit(solution)/shard_map/psum | solution.py:143
  265.1 2.0 convolution_convert_fusion.1
  267.2 1.8 copy.38
  270.1 1.7 constant_dynamic-update-slice_fusion.3
  271.8 25.4 %all-reduce.6.cloned.1.call-done = bf16[256,512]{0,1:T(8,128)(2,1)} async-done(((bf16[256,512]{0,1:T(8,128)(2,1)}), bf16[256,512]{0,1:T(8,128)(2,1)}) %all-reduce.6.cloned.1.call-update) | async-done | bytes 262160 | tf_op jit(solution)/shard_map/psum | solution.py:149
  298.7 1.8 copy.39
  300.5 1.8 copy.40
  302.3 1.7 constant_dynamic-update-slice_fusion.2
  304.0 1.7 constant_dynamic-update-slice_fusion.1
  305.7 1.8 copy.41
  307.5 1.7 constant_dynamic-update-slice_fusion
  311.5 1.7 multiply_convert_fusion
  314.9 3.6 fusion.44
  318.6 5.0 %fusion.42 = bf16[256,4096]{1,0:T(8,128)(2,1)} fusion(bf16[256,4096]{1,0:T(8,128)(2,1)S(1)} %copy-done, f32[256,4096]{1,0:T(8,128)S(1)} %fusion.44, bf16[256,512]{0,1:T(8,128)(2,1)S(1)} %bitcast.95, bf16[2,4096,512]{2,1,0:T(8,128)(2,1)} %param.21, pred[]{:T(512)S(6)} %lt.36), kind=kOutput, calls=%fused_computation.43 | convolution fusion | flops 1075838976 | bytes 12845057 | tf_op jit(solution)/shard_map/dot_general | solution.py:205
  323.7 25.7 %all-reduce.8.cloned.1.call-done = bf16[256,512]{1,0:T(8,128)(2,1)} async-done(((bf16[256,512]{1,0:T(8,128)(2,1)}), bf16[256,512]{1,0:T(8,128)(2,1)}) %all-reduce.8.cloned.1.call-update) | async-done | bytes 262160 | tf_op jit(solution)/shard_map/psum | solution.py:198
  349.4 72.4 %reduce-scatter.2.cloned.1.call-done = bf16[256,512]{1,0:T(8,128)(2,1)} async-done(((bf16[256,4096]{1,0:T(8,128)(2,1)}), bf16[256,512]{1,0:T(8,128)(2,1)}) %reduce-scatter.2.cloned.1.call-update) | async-done | bytes 262160 | tf_op jit(solution)/shard_map/reduce_scatter | solution.py:207
  421.8 2.0 broadcast_select_fusion
  (78 shorter events, 21.5 us)
Async XLA Ops:
  7.2 11.4 %copy-start.7 = (bf16[256,512]{1,0:T(8,128)(2,1)S(1)}, bf16[256,512]{1,0:T(8,128)(2,1)}, u32[]{:S(2)}) copy-start(bf16[256,512]{1,0:T(8,128)(2,1)} %param.16) | copy-start | bytes 786436
  7.2 11.4 %copy-start.10 = (s32[2,1024]{1,0:T(2,128)S(1)}, s32[2,1024]{1,0:T(2,128)}, u32[]{:S(2)}) copy-start(s32[2,1024]{1,0:T(2,128)} %param.22) | copy-start | bytes 24580
  7.2 11.4 %copy-start.11 = (s32[8]{0:T(128)S(1)}, s32[8]{0:T(128)}, u32[]{:S(2)}) copy-start(s32[8]{0:T(128)} %param.23) | copy-start | bytes 100
  7.2 22.9 %all-gather.6.cloned.1.call-start = ((), (), s32[]{:S(2)}) async-start(), calls=%async_computation.3 | async-start | bytes 1310720 | tf_op jit(solution)/shard_map/all_gather | solution.py:129
  7.9 74.9 %all-gather.8.cloned.1.call-start = ((), (), s32[]{:S(2)}) async-start(), calls=%async_computation.4 | async-start | bytes 2359296 | tf_op jit(solution)/shard_map/all_gather | solution.py:75
  8.7 178.3 %all-reduce.4.cloned.1.call-start = ((), (), s32[]{:S(2)}) async-start(), calls=%async_computation.2 | async-start | bytes 4194304 | tf_op jit(solution)/shard_map/psum | solution.py:105
  10.1 3.7 collective-permute-start
  12.5 5.5 %collective-permute-start.1 = (bf16[2,127,512]{1,2,0:T(8,128)(2,1)S(1)}, bf16[2,127,512]{1,2,0:T(8,128)(2,1)S(1)}, u32[]{:S(2)}, u32[]{:S(2)}) collective-permute-start(bf16[2,127,512]{1,2,0:T(8,128)(2,1)S(1)} %get-tuple-element.161), channel_id=1, source_target_pairs={{8,0},{16,8},{24,16},{9,1},{17,9},{25,17},{10,2},{18,10},{26,18},{... | collective-permute-start | bytes 780296 | tf_op jit(solution)/shard_map/ppermute | solution.py:41
  27.1 1.4 copy-start.2
  28.5 210.0 %all-gather.4.cloned.1.call-start = ((), (), s32[]{:S(2)}) async-start(), calls=%async_computation.1 | async-start | bytes 2359296 | tf_op jit(solution)/shard_map/all_gather | solution.py:74
  29.1 268.1 %all-reduce.6.cloned.1.call-start = ((), (), s32[]{:S(2)}) async-start(), calls=%async_computation.5 | async-start | bytes 524288 | tf_op jit(solution)/shard_map/psum | solution.py:149
  83.6 217.0 %collective-permute-start.3 = (bf16[256,512]{1,0:T(8,128)(2,1)}, bf16[256,512]{1,0:T(8,128)(2,1)}, u32[]{:S(2)}, u32[]{:S(2)}) collective-permute-start(bf16[256,512]{1,0:T(8,128)(2,1)} %get-tuple-element.171), channel_id=1, source_target_pairs={{0,24},{8,0},{16,8},{24,16},{1,25},{9,1},{17,9},{25,17},{2,26},{10... | collective-permute-start | bytes 786440 | tf_op jit(solution)/shard_map/ppermute | solution.py:24
  87.9 181.1 %collective-permute-start.2 = (bf16[256,512]{1,0:T(8,128)(2,1)}, bf16[256,512]{1,0:T(8,128)(2,1)}, u32[]{:S(2)}, u32[]{:S(2)}) collective-permute-start(bf16[256,512]{1,0:T(8,128)(2,1)} %get-tuple-element.171), channel_id=1, source_target_pairs={{0,8},{8,16},{16,24},{24,0},{1,9},{9,17},{17,25},{25,1},{2,10},{10... | collective-permute-start | bytes 786440 | tf_op jit(solution)/shard_map/ppermute | solution.py:19
  242.9 5.2 %copy-start.1 = (bf16[2,4096,512]{2,1,0:T(8,128)(2,1)S(1)}, bf16[2,4096,512]{2,1,0:T(8,128)(2,1)}, u32[]{:S(2)}) copy-start(bf16[2,4096,512]{2,1,0:T(8,128)(2,1)} %get-tuple-element.117) | copy-start | bytes 25165828 | tf_op jit(solution)/shard_map/cond
  251.4 6.6 %copy-start.3 = (bf16[256,8,64]{0,2,1:T(8,128)(2,1)}, bf16[256,8,64]{0,2,1:T(8,128)(2,1)S(1)}, u32[]{:S(2)}) copy-start(bf16[256,8,64]{0,2,1:T(8,128)(2,1)S(1)} %get-tuple-element.126) | copy-start | bytes 786436
  251.4 6.6 %copy-start.9 = (bf16[256,8,64]{0,2,1:T(8,128)(2,1)}, bf16[256,8,64]{0,2,1:T(8,128)(2,1)S(1)}, u32[]{:S(2)}) copy-start(bf16[256,8,64]{0,2,1:T(8,128)(2,1)S(1)} %get-tuple-element.127) | copy-start | bytes 786436
  267.0 82.4 %all-reduce.8.cloned.1.call-start = ((), (), s32[]{:S(2)}) async-start(), calls=%async_computation.7 | async-start | bytes 524288 | tf_op jit(solution)/shard_map/psum | solution.py:198
  269.0 36.8 %collective-permute-start.4 = (bf16[256,512]{1,0:T(8,128)(2,1)}, bf16[256,512]{1,0:T(8,128)(2,1)}, u32[]{:S(2)}, u32[]{:S(2)}) collective-permute-start(bf16[256,512]{1,0:T(8,128)(2,1)} %collective-permute-done.2), channel_id=1, source_target_pairs={{0,8},{8,16},{16,24},{24,0},{1,9},{9,17},{17,25},{25,1},{2,10},{10... | collective-permute-start | bytes 786440 | tf_op jit(solution)/shard_map/ppermute | solution.py:19
  311.5 1.7 copy-start.4
  314.8 107.0 %reduce-scatter.2.cloned.1.call-start = ((), (), s32[]{:S(2)}) async-start(), calls=%async_computation.6 | async-start | bytes 2359296 | tf_op jit(solution)/shard_map/reduce_scatter | solution.py:207
  314.9 3.7 copy-start
  314.9 3.7 copy-start.8
  318.6 103.3 %copy-start.5 = (bf16[256,512]{1,0:T(8,128)(2,1)S(1)}, bf16[256,512]{1,0:T(8,128)(2,1)}, u32[]{:S(2)}) copy-start(bf16[256,512]{1,0:T(8,128)(2,1)} %param.19) | copy-start | bytes 786436
  318.6 103.3 %copy-start.6 = (bf16[256,512]{1,0:T(8,128)(2,1)S(1)}, bf16[256,512]{1,0:T(8,128)(2,1)}, u32[]{:S(2)}) copy-start(bf16[256,512]{1,0:T(8,128)(2,1)} %param.18) | copy-start | bytes 786436
Sparse Core Ops, SparseCore 0:
  9.6 20.4 all-gather.5
  32.1 50.6 all-gather.7
  86.5 100.4 all-reduce.3
  188.9 49.6 all-gather.3
  267.2 29.9 all-reduce.5
  314.9 34.4 all-reduce.7
  352.9 68.8 reduce-scatter.1
